TPU v7x, 32 devices: a whole 2x2x4 slice. The times are simulated.
32 devices in a mesh: section: 4 (over y, x), student: 2 (over core), dp: 4 (over z).
Axes of the slice: x: 2, y: 2, z: 4, core: 2. Of those that a mesh axis runs over, the one named last changes fastest.
Arguments:
- in_flight: bfloat16 [4, 2, 128, 4096], P('section', 'student'), may hold values from -6 to 6
- segments: int32 [4, 2, 128], P(None, 'student'), may hold values from 0 to 3, never falling along the last dimension, each value on 1 to 64 neighbouring positions
- norm_gain: float32 [4, 4096], P('section'), may hold values from 0.5 to 1.5
- w_qkv: bfloat16 [4, 4096, 3, 1024], P('section', None, None, 'dp')
- w_out: bfloat16 [4, 1024, 4096], P('section', 'dp'), may hold values from -0.1875 to 0.1875
- final_gain: float32 [4096], replicated, may hold values from 0.25 to 1.75
- student_rows: bfloat16 [2, 3, 2, 128, 1024], P('student', None, None, 'dp'), may hold values from -6 to 6
- student_gain: float32 [2, 1024], P('student'), may hold values from 0.5 to 1.5
- w_head: bfloat16 [2, 1024, 4096], P('student', None, 'section'), may hold values from -0.1875 to 0.1875
Outputs:
- advanced: bfloat16 [4, 2, 128, 4096], P('section', 'student', 'dp')
- grad_head: float32 [2, 1024, 4096], P('student', 'dp', 'section')
Inputs may be any that keep to these rules, and one draw needn't show every extreme that they name: `segments`: along a micro-batch's tokens the crop numbers never fall; each of the 4 crops holds 1 to 64 tokens and one holds exactly 64.
All inputs are finite; a program needn't handle non-finite values.
Results may differ from a plain program's by a relative error of at most 0.025.
Values may be sent and summed in bfloat16 or wider, within the bound.
A program may use at most 64 MiB of HBM per device.

v0:
```python
import jax
import jax.numpy as jnp
from jax import lax
from jax.sharding import PartitionSpec as P

HEAD_SIZE = 128
TOK = 128


def shifted(x, axis, by):
    count = lax.axis_size(axis)
    pairs = [(i, i + by) for i in range(count) if 0 <= i + by < count]
    return lax.ppermute(x, axis, pairs)


def broadcast(value, axis, source):
    kept = jnp.where(lax.axis_index(axis) == source, value, 0).astype(value.dtype)
    return lax.psum(kept, axis)


def layer_norm(rows, gain):
    rows = rows.astype(jnp.float32)
    centred = rows - jnp.mean(rows, axis=-1, keepdims=True)
    spread = jnp.mean(centred * centred, axis=-1, keepdims=True)
    return centred * lax.rsqrt(spread + 1e-06) * gain


def attend(state, crops, gain, weights_qkv, weights_out):
    tokens = state.shape[0]
    width = weights_out.shape[0]
    heads = width // HEAD_SIZE
    normed = layer_norm(state, gain).astype(jnp.bfloat16)
    qkv = jnp.dot(normed, weights_qkv, preferred_element_type=jnp.float32).astype(jnp.bfloat16)
    query = qkv[:, :width].reshape(tokens, heads, HEAD_SIZE)
    keys = qkv[:, width : 2 * width].reshape(tokens, heads, HEAD_SIZE)
    values = qkv[:, 2 * width :].reshape(tokens, heads, HEAD_SIZE)
    scores = jnp.einsum(
        "qhd,khd->hqk", query, keys, preferred_element_type=jnp.float32
    ) * HEAD_SIZE ** (-0.5)
    same = crops[:, None] == crops[None, :]
    scores = jnp.where(same[None], scores, -1e30)
    top = jnp.max(scores, axis=-1, keepdims=True)
    expo = jnp.exp(scores - top)
    probs = (expo / jnp.sum(expo, axis=-1, keepdims=True)).astype(jnp.bfloat16)
    mixed = jnp.einsum("hqk,khd->qhd", probs, values, preferred_element_type=jnp.float32).astype(
        jnp.bfloat16
    )
    return jnp.dot(mixed.reshape(tokens, width), weights_out, preferred_element_type=jnp.float32)


def on_device(
    in_flight, segments, norm_gain, w_qkv, w_out, final_gain, student_rows, student_gain, w_head
):
    section = lax.axis_index("section")
    root = lax.axis_size("section") - 1
    share = in_flight.shape[2] // lax.axis_size("dp")
    first_row = lax.axis_index("dp") * share
    ticks = student_rows.shape[1]
    model_width = in_flight.shape[3]
    weights_qkv = w_qkv[0].reshape(model_width, -1)
    weights_out = w_out[0]
    gain = norm_gain[0]
    crop_table = segments[:, 0, :]
    finals = []
    whole = in_flight[0, 0]
    own_rows = lax.dynamic_slice_in_dim(whole, first_row, share, 0)
    for tick in range(ticks):
        if tick > 0:
            whole = lax.all_gather(own_rows, "dp", axis=0, tiled=True)
        crops = lax.dynamic_index_in_dim(crop_table, section - tick, 0, keepdims=False)
        partial_value = attend(whole, crops, gain, weights_qkv, weights_out)
        summed = lax.psum_scatter(
            partial_value.astype(jnp.bfloat16), "dp", scatter_dimension=0, tiled=True
        ).astype(jnp.float32)
        own_rows = (own_rows.astype(jnp.float32) + summed).astype(jnp.bfloat16)
        finals.append(layer_norm(own_rows, final_gain).astype(jnp.bfloat16))
        own_rows = shifted(own_rows, "section", 1)
    advanced = own_rows[None, None]
    finished = jnp.stack(finals)[:, None]
    block = w_head.shape[2]
    block_start = section * block
    columns = lax.all_gather(finished, "student", axis=1, tiled=True)
    spread_rows = broadcast(columns, "section", root)
    targets = lax.dynamic_slice_in_dim(spread_rows, block_start, block, 3)
    student_width = student_rows.shape[4]
    feats = (
        layer_norm(student_rows[0], student_gain[0]).astype(jnp.bfloat16).reshape(-1, student_width)
    )
    pred = jnp.dot(feats, w_head[0], preferred_element_type=jnp.float32)
    err = ((pred - targets.reshape(-1, block).astype(jnp.float32)) * (2.0 / TOK)).astype(
        jnp.bfloat16
    )
    term = lax.dot_general(feats, err, (((0,), (0,)), ((), ())), preferred_element_type=jnp.float32)
    grad = lax.psum_scatter(
        term.astype(jnp.bfloat16), "dp", scatter_dimension=0, tiled=True
    ).astype(jnp.float32)
    return (advanced, grad[None])


def solution(mesh):
    in_specs = (
        P("section", "student", None, None),
        P(None, "student", None),
        P("section", None),
        P("section", None, None, "dp"),
        P("section", "dp", None),
        P(),
        P("student", None, None, "dp", None),
        P("student", None),
        P("student", None, "section"),
    )
    out_specs = (P("section", "student", "dp", None), P("student", "dp", "section"))
    return jax.shard_map(
        on_device, mesh=mesh, in_specs=in_specs, out_specs=out_specs, check_vma=False
    )
```

profile of v0, /device:TPU:1, one launch (start us, length us, event | category | flops | bytes accessed | tf_op | source)
XLA Modules:
  0.0 339.8 jit_solution(15224556704318031938)
XLA Ops:
  8.2 8.9 %copy.23 = bf16[1,4096,3,256]{1,3,2,0:T(8,128)(2,1)} copy(bf16[1,4096,3,256]{3,1,2,0:T(8,128)(2,1)} %param.12) | data formatting | bytes 12582912 | tf_op args[3]
  17.8 5.0 %convolution_convert_fusion.6 = bf16[128,768]{1,0:T(8,128)(2,1)S(1)} fusion(bf16[4096,768]{0,1:T(8,128)(2,1)} %bitcast.129, bf16[1,1,128,4096]{3,2,1,0:T(8,128)(2,1)S(1)} %copy-done.2, f32[4096]{0:T(1024)S(1)} %bitcast.144, f32[128]{0:T(128)S(1)} %add_rsqrt_fusion.6, f32[128]{0:T(128)S(1)} %broadcast_multiply_fusion.6), kind=kOutput, calls=%fused_computation.41 | convolution fusion | flops 808026112 | bytes 7554048 | tf_op jit(solution)/shard_map/dot_general | solution.py:33
  24.9 29.1 %reduce-scatter.5.cloned.1.call-done = bf16[32,4096]{1,0:T(8,128)(2,1)} async-done(((bf16[128,4096]{1,0:T(8,128)(2,1)}), bf16[32,4096]{1,0:T(8,128)(2,1)}) %reduce-scatter.5.cloned.1.call-update) | async-done | bytes 262160 | tf_op jit(solution)/shard_map/reduce_scatter | solution.py:72
  55.1 3.1 collective-permute-start
  58.2 4.6 %collective-permute-done = bf16[32,4096]{1,0:T(8,128)(2,1)S(1)} collective-permute-done((bf16[32,4096]{1,0:T(8,128)(2,1)S(1)}, bf16[32,4096]{1,0:T(8,128)(2,1)S(1)}, u32[]{:S(2)}, u32[]{:S(2)}) %collective-permute-start) | collective-permute-done | bytes 262176 | tf_op jit(solution)/shard_map/ppermute | solution.py:13
  63.7 28.6 %all-gather.5.cloned.1.call-done = bf16[128,4096]{1,0:T(8,128)(2,1)} async-done(((bf16[32,4096]{1,0:T(8,128)(2,1)}), bf16[128,4096]{1,0:T(8,128)(2,1)}) %all-gather.5.cloned.1.call-update) | async-done | bytes 1048592 | tf_op jit(solution)/shard_map/all_gather | solution.py:69
  92.3 1.5 convert_reduce_fusion.2
  93.8 1.7 fusion.10
  95.5 5.0 %convolution_convert_fusion.5 = bf16[128,768]{1,0:T(8,128)(2,1)S(1)} fusion(bf16[4096,768]{0,1:T(8,128)(2,1)} %bitcast.130, bf16[128,4096]{1,0:T(8,128)(2,1)S(1)} %copy-done.3, f32[4096]{0:T(1024)S(1)} %bitcast.145, f32[128]{0:T(128)S(1)} %add_rsqrt_fusion.5, f32[128]{0:T(128)S(1)} %broadcast_multiply_fusion.5), kind=kOutput, calls=%fused_computation.40 | convolution fusion | flops 808026112 | bytes 7554048 | tf_op jit(solution)/shard_map/dot_general | solution.py:33
  102.6 26.9 %reduce-scatter.7.cloned.1.call-done = bf16[32,4096]{1,0:T(8,128)(2,1)} async-done(((bf16[128,4096]{1,0:T(8,128)(2,1)}), bf16[32,4096]{1,0:T(8,128)(2,1)}) %reduce-scatter.7.cloned.1.call-update) | async-done | bytes 262160 | tf_op jit(solution)/shard_map/reduce_scatter | solution.py:72
  130.6 3.1 collective-permute-start.1
  133.7 4.6 %collective-permute-done.1 = bf16[32,4096]{1,0:T(8,128)(2,1)S(1)} collective-permute-done((bf16[32,4096]{1,0:T(8,128)(2,1)S(1)}, bf16[32,4096]{1,0:T(8,128)(2,1)S(1)}, u32[]{:S(2)}, u32[]{:S(2)}) %collective-permute-start.1) | collective-permute-done | bytes 262176 | tf_op jit(solution)/shard_map/ppermute | solution.py:13
  139.1 28.7 %all-gather.7.cloned.1.call-done = bf16[128,4096]{1,0:T(8,128)(2,1)} async-done(((bf16[32,4096]{1,0:T(8,128)(2,1)}), bf16[128,4096]{1,0:T(8,128)(2,1)}) %all-gather.7.cloned.1.call-update) | async-done | bytes 1048592 | tf_op jit(solution)/shard_map/all_gather | solution.py:69
  167.8 1.5 convert_reduce_fusion.1
  169.3 1.7 fusion.7
  171.0 5.0 %convolution_convert_fusion.4 = bf16[128,768]{1,0:T(8,128)(2,1)S(1)} fusion(bf16[4096,768]{0,1:T(8,128)(2,1)} %bitcast.131, bf16[128,4096]{1,0:T(8,128)(2,1)S(1)} %copy-done.4, f32[128]{0:T(128)S(1)} %add_rsqrt_fusion.4, f32[128]{0:T(128)S(1)} %broadcast_multiply_fusion.4, f32[4096]{0:T(1024)S(1)} %bitcast.146), kind=kOutput, calls=%fused_computation.39 | convolution fusion | flops 808026112 | bytes 7554048 | tf_op jit(solution)/shard_map/dot_general | solution.py:33
  178.7 26.3 %reduce-scatter.9.cloned.1.call-done = bf16[32,4096]{1,0:T(8,128)(2,1)} async-done(((bf16[128,4096]{1,0:T(8,128)(2,1)}), bf16[32,4096]{1,0:T(8,128)(2,1)}) %reduce-scatter.9.cloned.1.call-update) | async-done | bytes 262160 | tf_op jit(solution)/shard_map/reduce_scatter | solution.py:72
  207.8 9.2 %all-gather.9.cloned.1.call-done = bf16[3,64,4096]{2,1,0:T(8,128)(2,1)} async-done(((bf16[3,32,4096]{2,1,0:T(8,128)(2,1)}), bf16[3,64,4096]{2,1,0:T(8,128)(2,1)}) %all-gather.9.cloned.1.call-update) | async-done | bytes 1572880 | tf_op jit(solution)/shard_map/all_gather | solution.py:82
  219.4 62.1 %all-reduce.2.cloned.1.call-done = bf16[3,2,32,4096]{3,2,1,0:T(8,128)(2,1)} async-done(((bf16[3,2,32,4096]{3,2,1,0:T(8,128)(2,1)}), bf16[3,2,32,4096]{3,2,1,0:T(8,128)(2,1)}) %all-reduce.2.cloned.1.call-update) | async-done | bytes 1572880 | tf_op jit(solution)/shard_map/psum | solution.py:18
  282.5 4.1 %convolution_convert_fusion.3 = bf16[1024,1024]{1,0:T(8,128)(2,1)} fusion(bf16[192,1024]{1,0:T(8,128)(2,1)S(1)} %fusion.62, bf16[192,1024]{1,0:T(8,128)(2,1)S(1)} %bitcast.133, bf16[1,1024,1024]{2,1,0:T(8,128)(2,1)} %param.17, bf16[192,1024]{1,0:T(8,128)(2,1)S(1)} %bitcast.134), kind=kOutput, calls=%fused_computation.34 | convolution fusion | flops 807141376 | bytes 5373952 | tf_op jit(solution)/shard_map/dot_general | solution.py:93
  286.6 3.1 collective-permute-start.2
  289.7 4.8 %collective-permute-done.2 = bf16[32,4096]{1,0:T(8,128)(2,1)S(1)} collective-permute-done((bf16[32,4096]{1,0:T(8,128)(2,1)S(1)}, bf16[32,4096]{1,0:T(8,128)(2,1)S(1)}, u32[]{:S(2)}, u32[]{:S(2)}) %collective-permute-start.2) | collective-permute-done | bytes 262176 | tf_op jit(solution)/shard_map/ppermute | solution.py:13
  294.5 35.6 %reduce-scatter.11.cloned.1.call-done = bf16[256,1024]{1,0:T(8,128)(2,1)} async-done(((bf16[1024,1024]{1,0:T(8,128)(2,1)}), bf16[256,1024]{1,0:T(8,128)(2,1)}) %reduce-scatter.11.cloned.1.call-update) | async-done | bytes 524304 | tf_op jit(solution)/shard_map/reduce_scatter | solution.py:94
  330.1 2.1 bitcast_convert_fusion
  (94 shorter events, 19.2 us)
Async XLA Ops:
  7.2 16.2 %copy-start = (bf16[1,256,4096]{2,1,0:T(8,128)(2,1)S(1)}, bf16[1,256,4096]{2,1,0:T(8,128)(2,1)}, u32[]{:S(2)}) copy-start(bf16[1,256,4096]{2,1,0:T(8,128)(2,1)} %param.13) | copy-start | bytes 6291460
  7.2 46.8 %reduce-scatter.5.cloned.1.call-start = ((), (), s32[]{:S(2)}) async-start(), calls=%async_computation.4 | async-start | bytes 1310720 | tf_op jit(solution)/shard_map/reduce_scatter | solution.py:72
  8.2 8.9 %copy-start.2 = (bf16[1,1,128,4096]{3,2,1,0:T(8,128)(2,1)S(1)}, bf16[1,1,128,4096]{3,2,1,0:T(8,128)(2,1)}, u32[]{:S(2)}) copy-start(bf16[1,1,128,4096]{3,2,1,0:T(8,128)(2,1)} %param.9) | copy-start | bytes 3145732
  17.1 0.7 copy-start.11
  24.8 67.4 %all-gather.5.cloned.1.call-start = ((), (), s32[]{:S(2)}) async-start(), calls=%async_computation.5 | async-start | bytes 1310720 | tf_op jit(solution)/shard_map/all_gather | solution.py:69
  55.1 7.7 %collective-permute-start = (bf16[32,4096]{1,0:T(8,128)(2,1)S(1)}, bf16[32,4096]{1,0:T(8,128)(2,1)S(1)}, u32[]{:S(2)}, u32[]{:S(2)}) collective-permute-start(bf16[32,4096]{1,0:T(8,128)(2,1)S(1)} %get-tuple-element.3), channel_id=1, source_target_pairs={{0,8},{8,16},{16,24},{1,9},{9,17},{17,25},{2,10},{10,18},{18,26},{... | collective-permute-start | bytes 786440 | tf_op jit(solution)/shard_map/ppermute | solution.py:13
  62.8 0.7 copy-start.7
  63.5 66.0 %reduce-scatter.7.cloned.1.call-start = ((), (), s32[]{:S(2)}) async-start(), calls=%async_computation.6 | async-start | bytes 1310720 | tf_op jit(solution)/shard_map/reduce_scatter | solution.py:72
  92.3 3.2 copy-start.3
  101.1 28.4 %copy-start.8 = (bf16[32,4096]{1,0:T(8,128)(2,1)S(1)}, bf16[32,4096]{1,0:T(8,128)(2,1)}, u32[]{:S(2)}) copy-start(bf16[32,4096]{1,0:T(8,128)(2,1)} %copy-done.7) | copy-start | bytes 786436
  102.6 65.2 %all-gather.7.cloned.1.call-start = ((), (), s32[]{:S(2)}) async-start(), calls=%async_computation.7 | async-start | bytes 1310720 | tf_op jit(solution)/shard_map/all_gather | solution.py:69
  130.6 7.7 %collective-permute-start.1 = (bf16[32,4096]{1,0:T(8,128)(2,1)S(1)}, bf16[32,4096]{1,0:T(8,128)(2,1)S(1)}, u32[]{:S(2)}, u32[]{:S(2)}) collective-permute-start(bf16[32,4096]{1,0:T(8,128)(2,1)S(1)} %get-tuple-element.5), channel_id=1, source_target_pairs={{0,8},{8,16},{16,24},{1,9},{9,17},{17,25},{2,10},{10,18},{18,26},{... | collective-permute-start | bytes 786440 | tf_op jit(solution)/shard_map/ppermute | solution.py:13
  138.3 0.7 copy-start.5
  139.0 66.0 %reduce-scatter.9.cloned.1.call-start = ((), (), s32[]{:S(2)}) async-start(), calls=%async_computation.8 | async-start | bytes 1310720 | tf_op jit(solution)/shard_map/reduce_scatter | solution.py:72
  167.8 3.2 copy-start.4
  176.6 28.4 %copy-start.6 = (bf16[32,4096]{1,0:T(8,128)(2,1)S(1)}, bf16[32,4096]{1,0:T(8,128)(2,1)}, u32[]{:S(2)}) copy-start(bf16[32,4096]{1,0:T(8,128)(2,1)} %copy-done.5) | copy-start | bytes 786436
  178.1 28.3 %copy-start.9 = (f32[4096]{0:T(1024)S(1)}, f32[4096]{0:T(1024)}, u32[]{:S(2)}) copy-start(f32[4096]{0:T(1024)} %param.14) | copy-start | bytes 49156
  178.1 38.8 %all-gather.9.cloned.1.call-start = ((), (), s32[]{:S(2)}) async-start(), calls=%async_computation.11 | async-start | bytes 2359296 | tf_op jit(solution)/shard_map/all_gather | solution.py:82
  207.7 73.7 %all-reduce.2.cloned.1.call-start = ((), (), s32[]{:S(2)}) async-start(), calls=%async_computation.9 | async-start | bytes 3145728 | tf_op jit(solution)/shard_map/psum | solution.py:18
  207.8 10.5 %copy-start.1 = (bf16[1,3,2,32,1024]{4,3,2,1,0:T(8,128)(2,1)S(1)}, bf16[1,3,2,32,1024]{4,3,2,1,0:T(8,128)(2,1)}, u32[]{:S(2)}) copy-start(bf16[1,3,2,32,1024]{4,3,2,1,0:T(8,128)(2,1)} %param.15) | copy-start | bytes 1179652
  207.8 11.1 %copy-start.10 = (f32[1,1024]{1,0:T(1,128)S(1)}, f32[1,1024]{1,0:T(1,128)}, u32[]{:S(2)}) copy-start(f32[1,1024]{1,0:T(1,128)} %param.16) | copy-start | bytes 12292
  218.2 111.9 %reduce-scatter.11.cloned.1.call-start = ((), (), s32[]{:S(2)}) async-start(), calls=%async_computation.10 | async-start | bytes 2621440 | tf_op jit(solution)/shard_map/reduce_scatter | solution.py:94
  286.6 7.9 %collective-permute-start.2 = (bf16[32,4096]{1,0:T(8,128)(2,1)S(1)}, bf16[32,4096]{1,0:T(8,128)(2,1)S(1)}, u32[]{:S(2)}, u32[]{:S(2)}) collective-permute-start(bf16[32,4096]{1,0:T(8,128)(2,1)S(1)} %get-tuple-element.7), channel_id=1, source_target_pairs={{0,8},{8,16},{16,24},{1,9},{9,17},{17,25},{2,10},{10,18},{18,26},{... | collective-permute-start | bytes 786440 | tf_op jit(solution)/shard_map/ppermute | solution.py:13
Sparse Core Ops, SparseCore 0:
  25.0 28.9 reduce-scatter.4
  63.6 28.5 all-gather.4
  102.7 26.7 reduce-scatter.6
  139.1 28.5 all-gather.6
  178.2 26.7 reduce-scatter.8
  207.8 9.0 all-gather.8
  220.0 61.3 all-reduce.1
  286.7 43.3 reduce-scatter.10
where the time goes:
time: 342 us; the launch traced here: 340 us
  waiting for transfers between devices  260 us (76%)
  matrix products  24.5 us (7%)
  other arithmetic  17.2 us (5%)
  between operations  14.5 us (4%)
  local copies, waits for them, and re-layouts  13.5 us (4%)
  starting transfers between devices  9.64 us (3%)
    reduce_scatter x3, waiting for transfers between devices, on_device(): lax.psum_scatter(partial_value.astype(jnp.bfloat16), 'dp', scatter_dimens...  82.2 us
    psum x1, waiting for transfers between devices, broadcast(): return lax.psum(kept, axis)  62.1 us
    all_gather x2, waiting for transfers between devices, on_device(): whole = lax.all_gather(own_rows, 'dp', axis=0, tiled=True)  57.3 us
    reduce_scatter x1, waiting for transfers between devices, on_device(): lax.psum_scatter(term.astype(jnp.bfloat16), 'dp', scatter_dimension=0, ti...  35.6 us
    dot_general x3, matrix products, attend(): jnp.dot(normed, weights_qkv, preferred_element_type=jnp.float32)  15.1 us
    ppermute x3, waiting for transfers between devices, shifted(): return lax.ppermute(x, axis, pairs)  13.9 us
    unnamed x29, local copies, waits for them, and re-layouts  11.1 us
    ppermute x3, starting transfers between devices, shifted(): return lax.ppermute(x, axis, pairs)  9.31 us
  transfers between devices with their start and end apart: 11, of which 11 were waited for; matrix products, arithmetic and copies ran while one was open for 0% of the time, Pallas kernels for 0%

commit v1 on v0

v1 whole, which is shorter than its diff:
```python
import functools

import jax
import jax.numpy as jnp
from jax import lax
from jax.experimental import pallas as pl
from jax.experimental.pallas import tpu as pltpu
from jax.sharding import PartitionSpec as P

HEAD_SIZE = 128
LN_ROWS = 16
BF16 = jnp.bfloat16
F32 = jnp.float32
MESH = pl.DeviceIdType.MESH


def layer_norm(rows, gain):
    rows = rows.astype(F32)
    centred = rows - jnp.mean(rows, axis=-1, keepdims=True)
    spread = jnp.mean(centred * centred, axis=-1, keepdims=True)
    return centred * lax.rsqrt(spread + 1e-06) * gain


def attend(query, keys, values, same):
    scores = lax.dot_general(
        query, keys, (((1,), (1,)), ((), ())), preferred_element_type=F32
    ) * HEAD_SIZE ** (-0.5)
    scores = jnp.where(same, scores, -1e30)
    top = jnp.max(scores, axis=-1, keepdims=True)
    expo = jnp.exp(scores - top)
    probs = (expo / jnp.sum(expo, axis=-1, keepdims=True)).astype(BF16)
    return jnp.dot(probs, values, preferred_element_type=F32).astype(BF16)


def window_kernel(
    S, M, Z, T, R,
    x_ref, seg_ref, gain_ref, wqkv_ref, wout_ref, fgain_ref, srows_ref, sgain_ref, whead_ref,
    adv_ref, grad_ref,
    wqkv, wofull, whead, normed, xfull, mixfull, xs, xrows, fin, tg, tbuf, advbuf,
    feats, pred, ffull, errfull,
    local_sem, wo_s, wo_r, wf_s, wf_r, mx_s, mx_r, sh_s, sh_r, ar_s, ar_r, al_s, al_r,
    ro_s, ro_r, ad_s, ad_r, tg_s, tg_r, fe_s, fe_r, er_s, er_r,
):
    s = lax.axis_index("section")
    c = lax.axis_index("student")
    z = lax.axis_index("dp")
    root = S - 1
    tokens, model = x_ref.shape
    wid = wout_ref.shape[0]
    share = tokens // Z
    cw = model // Z
    block = whead_ref.shape[1]
    sw = whead_ref.shape[0]
    fw = sw // Z
    step_rows = tokens // R
    halves = 2 if M % 2 == 0 else 1
    part = c % halves
    hw = wid // halves
    sends = []

    def remote(src, dst, send, recv, where):
        return pltpu.make_async_remote_copy(
            src_ref=src, dst_ref=dst, send_sem=send, recv_sem=recv,
            device_id=where, device_id_type=MESH,
        )

    def post(cond, build):
        if cond is True:
            build().start()
        else:
            pl.when(cond)(lambda: build().start())
        sends.append((cond, build))

    def zmod(value):
        return lax.rem(value + Z, Z)

    def cols(index):
        return pl.ds(pl.multiple_of(index * cw, 128), cw)

    load_qkv = pltpu.make_async_copy(wqkv_ref, wqkv, local_sem.at[0])
    load_head = pltpu.make_async_copy(whead_ref, whead, local_sem.at[1])
    own_wo = pltpu.make_async_copy(
        wout_ref.at[:, cols(z)],
        wofull.at[pl.ds(pl.multiple_of(z * wid, wid), wid), :],
        local_sem.at[2],
    )
    load_qkv.start()
    own_wo.start()
    load_head.start()

    barrier = pltpu.get_barrier_semaphore()

    def greet(where):
        pl.semaphore_signal(barrier, inc=1, device_id=where, device_id_type=MESH)

    for k in range(1, Z):
        greet((s, c, zmod(z + k)))
    for k in range(Z):
        pl.when(s > 0)(functools.partial(greet, (s - 1, c, zmod(z + k))))
        pl.when(s < root)(functools.partial(greet, (s + 1, c, zmod(z + k))))
    for at in range(S):
        far = jnp.logical_or(s - at > 1, at - s > 1)
        pl.when(far)(functools.partial(greet, (jnp.int32(at), c, z)))
        for dm in range(1, M):
            greet((jnp.int32(at), lax.rem(c + dm, M), z))
    for at in range(S):
        near = min(at, 1) + min(root - at, 1)
        peers = (Z - 1) + Z * near + (S - 1 - near) + S * (M - 1)
        pl.when(s == at)(functools.partial(pl.semaphore_wait, barrier, peers))

    def wo_rows(source, which):
        return pl.ds(pl.multiple_of(source * wid + which * hw, hw), hw)

    for k in sorted(range(1, Z), reverse=True):
        def build(k=k):
            to = zmod(z + k)
            return remote(
                wout_ref.at[pl.ds(pl.multiple_of(part * hw, hw), hw), cols(to)],
                wofull.at[wo_rows(z, part), :],
                wo_s.at[k - 1], wo_r.at[k - 1], (s, c, to),
            )
        post(True, build)

    def pass_on(k):
        source = zmod(z - k)
        mine = wofull.at[wo_rows(source, part), :]
        mate = c + 1 - 2 * part
        return remote(mine, mine, wf_s.at[k - 1], wf_r.at[k - 1], (s, mate, z))

    def gather_wo():
        for k in range(1, Z):
            source = zmod(z - k)
            mine = wofull.at[wo_rows(source, part), :]
            remote(mine, mine, wo_s.at[k - 1], wo_r.at[k - 1], (s, c, source)).wait_recv()
            if halves == 2:
                post(True, functools.partial(pass_on, k))
        if halves == 2:
            for k in range(1, Z):
                source = zmod(z - k)
                other = wofull.at[wo_rows(source, 1 - part), :]
                remote(other, other, wf_s.at[k - 1], wf_r.at[k - 1],
                       (s, c + 1 - 2 * part, z)).wait_recv()
        own_wo.wait()

    def student():
        rows = layer_norm(srows_ref[...].astype(F32).reshape(T * M * share, sw), sgain_ref[...])
        rows = rows.astype(BF16)
        for zz in range(Z):
            feats[zz] = rows[:, zz * fw:(zz + 1) * fw].reshape(T, M * share, fw)
        for k in range(1, Z):
            def build(k=k):
                to = zmod(z + k)
                return remote(feats.at[to], ffull.at[z], fe_s.at[k - 1], fe_r.at[k - 1], (s, c, to))
            post(True, build)
        ffull[z] = feats[z]
        load_head.wait()
        pred[...] = jnp.dot(rows, whead[...], preferred_element_type=F32).reshape(
            T, M, share, block
        )

    def errors(t):
        for cs in range(M):
            def take(cs=cs):
                there = tbuf.at[t, cs]
                remote(there, there, tg_s.at[t, 0], tg_r.at[t, cs], (root, cs, z)).wait_recv()
            pl.when(jnp.logical_or(s != root, c != cs))(take)
        err = (pred[t] - tbuf[t].astype(F32)) * (2.0 / tokens)
        errfull[t, z] = err.reshape(M * share, block).astype(BF16)
        for k in range(1, Z):
            def build(k=k):
                own = errfull.at[t, z]
                return remote(own, own, er_s.at[t, k - 1], er_r.at[t, k - 1],
                              (s, c, zmod(z + k)))
            post(True, build)

    def gradient(t):
        for k in range(1, Z):
            there = errfull.at[t, zmod(z - k)]
            remote(there, there, er_s.at[t, k - 1], er_r.at[t, k - 1],
                   (s, c, zmod(z - k))).wait_recv()
        term = lax.dot_general(
            ffull[:, t].reshape(Z * M * share, fw), errfull[t].reshape(Z * M * share, block),
            (((0,), (0,)), ((), ())), preferred_element_type=F32,
        )
        if t == 0:
            grad_ref[...] = term
        else:
            grad_ref[...] += term

    def take_feats():
        for k in range(1, Z):
            there = ffull.at[zmod(z - k)]
            remote(there, there, fe_s.at[k - 1], fe_r.at[k - 1], (s, c, zmod(z - k))).wait_recv()

    def gather_state(t, active):
        def piece(r, origin):
            return xfull.at[t - 1, pl.ds(r * step_rows, step_rows), cols(origin)]

        def to_right(r, k):
            there = piece(r, z - k)
            return remote(there, there, ar_s.at[t - 1, k, r], ar_r.at[t - 1, k, r], (s, c, z + 1))

        def to_left(r, k):
            there = piece(r, z + k)
            return remote(there, there, al_s.at[t - 1, k, r], al_r.at[t - 1, k, r], (s, c, z - 1))

        def right_from(r, k):
            there = piece(r, z - k)
            remote(there, there, ar_s.at[t - 1, k - 1, r], ar_r.at[t - 1, k - 1, r],
                   (s, c, z - 1)).wait_recv()

        def left_from(r, k):
            there = piece(r, z + k)
            remote(there, there, al_s.at[t - 1, k - 1, r], al_r.at[t - 1, k - 1, r],
                   (s, c, z + 1)).wait_recv()

        for r in range(R):
            def first(r=r):
                there = piece(r, z)
                remote(there, there, sh_s.at[t - 1, r], sh_r.at[t - 1, r],
                       (s - 1, c, z)).wait_recv()
            pl.when(active)(first)
            post(jnp.logical_and(active, z < Z - 1), functools.partial(to_right, r, 0))
            post(jnp.logical_and(active, z > 0), functools.partial(to_left, r, 0))
        for k in range(1, Z):
            for r in range(R):
                pl.when(jnp.logical_and(active, z >= k))(functools.partial(right_from, r, k))
                if k < Z - 1:
                    post(jnp.logical_and(active, jnp.logical_and(z >= k, z < Z - 1)),
                         functools.partial(to_right, r, k))
                pl.when(jnp.logical_and(active, z + k < Z))(functools.partial(left_from, r, k))
                if k < Z - 1:
                    post(jnp.logical_and(active, jnp.logical_and(z + k < Z, z > 0)),
                         functools.partial(to_left, r, k))

    def mix_cols(index):
        return pl.ds(pl.multiple_of(index * wid, 128), wid)

    def mixing(t):
        source = x_ref if t == 0 else xfull.at[t - 1]

        def norm_rows(i, carry):
            rows = pl.ds(pl.multiple_of(i * LN_ROWS, LN_ROWS), LN_ROWS)
            normed[rows, :] = layer_norm(source[rows, :], gain_ref[...]).astype(BF16)
            return carry

        lax.fori_loop(0, tokens // LN_ROWS, norm_rows, 0)
        if t == 0:
            load_qkv.wait()
        rows = normed[...]
        query, keys, values = [
            jnp.dot(rows, wqkv[:, j * wid:(j + 1) * wid], preferred_element_type=F32).astype(BF16)
            for j in range(3)
        ]
        crops = jnp.broadcast_to(seg_ref[s - t].astype(F32), (tokens, tokens))
        same = crops == crops.T
        outs = []
        for h in range(wid // HEAD_SIZE):
            at = slice(h * HEAD_SIZE, (h + 1) * HEAD_SIZE)
            outs.append(attend(query[:, at], keys[:, at], values[:, at], same))
        mixfull[t, :, mix_cols(z)] = jnp.concatenate(outs, axis=1)

    def send_mixed(t, active):
        for k in range(1, Z):
            def build(k=k):
                own = mixfull.at[t, :, mix_cols(z)]
                return remote(own, own, mx_s.at[t, k - 1], mx_r.at[t, k - 1],
                              (s, c, zmod(z + k)))
            post(active, build)

    def project(t):
        for k in range(1, Z):
            there = mixfull.at[t, :, mix_cols(zmod(z - k))]
            remote(there, there, mx_s.at[t, k - 1], mx_r.at[t, k - 1],
                   (s, c, zmod(z - k))).wait_recv()
        own = x_ref[:, cols(z)] if t == 0 else xfull[t - 1, :, cols(z)]
        summed = own.astype(F32) + jnp.dot(mixfull[t], wofull[...], preferred_element_type=F32)
        if t < T - 1:
            xs[t] = summed.astype(BF16)
        xrows[t] = summed.reshape(Z, share, cw).astype(BF16)

    def send_state(t, active):
        if t < T - 1:
            for r in range(R):
                def build(r=r):
                    at = pl.ds(r * step_rows, step_rows)
                    return remote(xs.at[t, at, :], xfull.at[t, at, cols(z)],
                                  sh_s.at[t, r], sh_r.at[t, r], (s + 1, c, z))
                post(jnp.logical_and(active, s < root), build)
        else:
            for k in range(Z):
                def build(k=k):
                    to = zmod(z + k)
                    return remote(xrows.at[t, to], advbuf.at[:, cols(z)],
                                  ad_s.at[k], ad_r.at[k], (s + 1, c, to))
                post(jnp.logical_and(active, s < root), build)
        for k in range(1, Z):
            def build_row(k=k):
                to = zmod(z + k)
                return remote(xrows.at[t, to], fin.at[t, :, cols(z)],
                              ro_s.at[t, k - 1], ro_r.at[t, k - 1], (s, c, to))
            post(s == root, build_row)

    def finish(t):
        def rows():
            fin[t, :, cols(z)] = xrows[t, z]
            for k in range(1, Z):
                there = fin.at[t, :, cols(zmod(z - k))]
                remote(there, there, ro_s.at[t, k - 1], ro_r.at[t, k - 1],
                       (s, c, zmod(z - k))).wait_recv()
            tg[t] = layer_norm(fin[t], fgain_ref[...]).astype(BF16)
            tbuf[t, c] = tg[t, :, root * block:(root + 1) * block]

        pl.when(s == root)(rows)
        for to in range(S):
            for dm in range(M):
                if to == root and dm == 0:
                    continue

                def build(to=to, dm=dm):
                    return remote(
                        tg.at[t, :, to * block:(to + 1) * block], tbuf.at[t, c],
                        tg_s.at[t, to * M + dm], tg_r.at[t, c],
                        (jnp.int32(to), lax.rem(c + dm, M), z),
                    )
                post(s == root, build)

    for t in range(T):
        active = True if t == 0 else s >= t
        if t == 0:
            mixing(0)
        else:
            gather_state(t, active)
            pl.when(active)(functools.partial(mixing, t))
        send_mixed(t, active)
        if t == 0:
            student()
            gather_wo()
            project(0)
        else:
            errors(t - 1)
            pl.when(active)(functools.partial(project, t))
        send_state(t, active)
        finish(t)

    take_feats()
    for t in range(T - 1):
        gradient(t)
    errors(T - 1)
    gradient(T - 1)

    def arrived():
        for k in range(Z):
            there = advbuf.at[:, cols(zmod(z - k))]
            remote(there, there, ad_s.at[k], ad_r.at[k], (s - 1, c, zmod(z - k))).wait_recv()
        adv_ref[...] = advbuf[...]

    def nothing():
        adv_ref[...] = jnp.zeros_like(adv_ref)

    pl.when(s >= T)(arrived)
    pl.when(s < T)(nothing)
    for cond, build in sends:
        if cond is True:
            build().wait_send()
        else:
            pl.when(cond)(lambda build=build: build().wait_send())


def solution(mesh):
    S, M, Z = mesh.shape["section"], mesh.shape["student"], mesh.shape["dp"]

    def on_device(
        in_flight, segments, norm_gain, w_qkv, w_out, final_gain, student_rows, student_gain, w_head
    ):
        tokens, model = in_flight.shape[2:]
        wid = w_out.shape[1]
        T, share = student_rows.shape[1], tokens // Z
        sw, block = w_head.shape[1:]
        cw, fw = model // Z, sw // Z
        R = 4 if Z <= 4 else 2
        vmem = pl.BlockSpec(memory_space=pltpu.VMEM)
        hbm = pl.BlockSpec(memory_space=pl.ANY)
        dma = pltpu.SemaphoreType.DMA
        K = max(Z - 1, 1)
        adv, grad = pl.pallas_call(
            functools.partial(window_kernel, S, M, Z, T, R),
            out_shape=(
                jax.ShapeDtypeStruct((share, model), BF16),
                jax.ShapeDtypeStruct((fw, block), F32),
            ),
            in_specs=[vmem, vmem, vmem, hbm, hbm, vmem, vmem, vmem, hbm],
            out_specs=(vmem, vmem),
            scratch_shapes=[
                pltpu.VMEM((model, 3 * wid), BF16),
                pltpu.VMEM((Z * wid, cw), BF16),
                pltpu.VMEM((sw, block), BF16),
                pltpu.VMEM((tokens, model), BF16),
                pltpu.VMEM((T - 1, tokens, model), BF16),
                pltpu.VMEM((T, tokens, Z * wid), BF16),
                pltpu.VMEM((T - 1, tokens, cw), BF16),
                pltpu.VMEM((T, Z, share, cw), BF16),
                pltpu.VMEM((T, share, model), BF16),
                pltpu.VMEM((T, share, model), BF16),
                pltpu.VMEM((T, M, share, block), BF16),
                pltpu.VMEM((share, model), BF16),
                pltpu.VMEM((Z, T, M * share, fw), BF16),
                pltpu.VMEM((T, M, share, block), F32),
                pltpu.VMEM((Z, T, M * share, fw), BF16),
                pltpu.VMEM((T, Z, M * share, block), BF16),
                dma((3,)),
                dma((K,)), dma((K,)), dma((K,)), dma((K,)),
                dma((T, K)), dma((T, K)),
                dma((T - 1, R)), dma((T - 1, R)),
                dma((T - 1, K, R)), dma((T - 1, K, R)),
                dma((T - 1, K, R)), dma((T - 1, K, R)),
                dma((T, K)), dma((T, K)),
                dma((Z,)), dma((Z,)),
                dma((T, S * M)), dma((T, M)),
                dma((K,)), dma((K,)),
                dma((T, K)), dma((T, K)),
            ],
            compiler_params=pltpu.CompilerParams(
                collective_id=0, has_side_effects=True, vmem_limit_bytes=58 << 20
            ),
        )(
            in_flight[0, 0], segments, norm_gain, w_qkv[0].reshape(model, -1), w_out[0],
            final_gain[None], student_rows[0], student_gain, w_head[0],
        )
        return adv[None, None], grad[None]

    in_specs = (
        P("section", "student", None, None),
        P(None, "student", None),
        P("section", None),
        P("section", None, None, "dp"),
        P("section", "dp", None),
        P(),
        P("student", None, None, "dp", None),
        P("student", None),
        P("student", None, "section"),
    )
    out_specs = (P("section", "student", "dp", None), P("student", "dp", "section"))
    return jax.shard_map(
        on_device, mesh=mesh, in_specs=in_specs, out_specs=out_specs, check_vma=False
    )
```

time: 342 us -> 172 us (0.50)
  waiting for transfers between devices: 260 us -> 0 us
  Pallas kernels: 0 us -> 148 us
  matrix products: 24.5 us -> 0 us
  other arithmetic: 17.2 us -> 0 us
  between operations: 14.5 us -> 0.64 us
  starting transfers between devices: 9.64 us -> 0 us
  local copies, waits for them, and re-layouts: 13.5 us -> 21.4 us
    pallas_call x0 -> x1, Pallas kernels: none -> 148 us  [on_device(): pl.pallas_call(functools.partial(window_kernel, S, M, Z, T, R), out_shape...]
    reduce_scatter x4 -> x0, waiting for transfers between devices: 118 us -> none  [the longest x3 82.2 us: on_device(): lax.psum_scatter(partial_value.astype(jnp.bfloat16), 'dp', scatter_dimens...]
    all_gather x3 -> x0, waiting for transfers between devices: 66.5 us -> none  [the longest x2 57.3 us: on_device(): whole = lax.all_gather(own_rows, 'dp', axis=0, tiled=True)]
    psum x1 -> x0, waiting for transfers between devices: 62.1 us -> none  [broadcast(): return lax.psum(kept, axis)]
    dot_general x13 -> x0, matrix products: 24.5 us -> none  [the longest x3 15.1 us: attend(): jnp.dot(normed, weights_qkv, preferred_element_type=jnp.float32)]
    ppermute x3 -> x0, waiting for transfers between devices: 13.9 us -> none  [shifted(): return lax.ppermute(x, axis, pairs)]
    reduce_sum x14 -> x0, other arithmetic: 11.6 us -> none  [the longest x7 6.85 us: layer_norm(): centred = rows - jnp.mean(rows, axis=-1, keepdims=True)]
    ppermute x3 -> x0, starting transfers between devices: 9.31 us -> none  [shifted(): return lax.ppermute(x, axis, pairs)]
  transfers between devices with their start and end apart: 11 -> 0, of which waited for: 11 -> 0; matrix products, arithmetic and copies ran while one was open for 0% -> 0% of each run, Pallas kernels for 0% -> 0%
where the time goes in v1:
time: 172 us; the launch traced here: 170 us
  Pallas kernels  148 us (86%)
  local copies, waits for them, and re-layouts  21.4 us (12%)
    pallas_call x1, Pallas kernels, on_device(): pl.pallas_call(functools.partial(window_kernel, S, M, Z, T, R), out_shape...  148 us
    unnamed x3, local copies, waits for them, and re-layouts  12.7 us
    another operation x1, local copies, waits for them, and re-layouts, on_device(): w_qkv[0].reshape(model, -1)  8.67 us

profile of v1, /device:TPU:1, one launch (start us, length us, event | category | flops | bytes accessed | tf_op | source)
XLA Modules:
  0.0 170.0 jit_solution(3328415233177764367)
XLA Ops:
  0.6 8.8 %copy.12 = bf16[1,4096,3,256]{1,3,2,0:T(8,128)(2,1)} copy(bf16[1,4096,3,256]{3,1,2,0:T(8,128)(2,1)} %param.12) | data formatting | bytes 12582912 | tf_op args[3]
  9.4 8.7 %copy.13.wqkv_ref = bf16[4096,768]{1,0:T(8,128)(2,1)} copy(bf16[4096,768]{0,1:T(8,128)(2,1)} %bitcast.8) | data formatting | bytes 12582912 | tf_op jit(solution)/shard_map/reshape;squeeze | solution.py:427
  18.1 147.9 %shard_map.104 = (bf16[32,4096]{1,0:T(8,128)(2,1)}, f32[256,1024]{1,0:T(8,128)}) custom-call(bf16[128,4096]{1,0:T(8,128)(2,1)} %bitcast.11, s32[4,1,128]{2,1,0:T(1,128)} %seg_ref.1, f32[1,4096]{1,0:T(1,128)} %gain_ref.1, bf16[4096,768]{1,0:T(8,128)(2,1)} %copy.13.wqkv_ref, bf16[256,4096]{1,0:T(8,128)(2,1)} %bitcast.9, f32[1,4096]{1,0:T(1,128)} %bitcast.15, ...), custom_call_target="tpu_custom_call" | custom-call | tf_op jit(solution)/shard_map/pallas_call | solution.py:386
  166.0 1.7 copy.16
  167.7 2.3 %copy.17 = f32[1,256,1024]{2,1,0:T(8,128)} copy(f32[1,256,1024]{2,1,0:T(8,128)} %bitcast.12) | data formatting | bytes 2097152

commit v2 on v1

--- a/solution.py
+++ b/solution.py
@@ -37,9 +37,10 @@
     x_ref, seg_ref, gain_ref, wqkv_ref, wout_ref, fgain_ref, srows_ref, sgain_ref, whead_ref,
     adv_ref, grad_ref,
     wqkv, wofull, whead, normed, xfull, mixfull, xs, xrows, fin, tg, tbuf, advbuf,
-    feats, pred, ffull, errfull,
+    sall, pred, fown, errs,
     local_sem, wo_s, wo_r, wf_s, wf_r, mx_s, mx_r, sh_s, sh_r, ar_s, ar_r, al_s, al_r,
-    ro_s, ro_r, ad_s, ad_r, tg_s, tg_r, fe_s, fe_r, er_s, er_r,
+    ro_s, ro_r, ad_s, ad_r, tg_s, tg_r, fe_s, fe_r, fp_s, fp_r,
+    er_s, er_r, ml_s, ml_r,
 ):
     s = lax.axis_index("section")
     c = lax.axis_index("student")
@@ -52,6 +53,7 @@
     block = whead_ref.shape[1]
     sw = whead_ref.shape[0]
     fw = sw // Z
+    ow = sw // S
     step_rows = tokens // R
     halves = 2 if M % 2 == 0 else 1
     part = c % halves
@@ -142,55 +144,95 @@
                        (s, c + 1 - 2 * part, z)).wait_recv()
         own_wo.wait()
 
+    def scols(index):
+        return pl.ds(pl.multiple_of(index * ow, 128), ow)
+
+    def spread_rows():
+        sall[0] = srows_ref[...]
+        for k in range(1, Z):
+            def build(k=k):
+                return remote(srows_ref.at[:, :, :, scols(s)], sall.at[k, :, :, :, scols(s)],
+                              fe_s.at[k - 1], fe_r.at[k - 1], (s, c, zmod(z + k)))
+            post(True, build)
+
+    def pass_rows():
+        for k in range(1, Z):
+            there = sall.at[k, :, :, :, scols(s)]
+            remote(there, there, fe_s.at[k - 1], fe_r.at[k - 1], (s, c, zmod(z - k))).wait_recv()
+        for k in range(1, S):
+            def build(k=k):
+                there = sall.at[pl.ds(1, Z - 1), :, :, :, scols(s)]
+                return remote(there, there, fp_s.at[k - 1], fp_r.at[k - 1],
+                              (lax.rem(s + k, S), c, z))
+            post(True, build)
+
     def student():
-        rows = layer_norm(srows_ref[...].astype(F32).reshape(T * M * share, sw), sgain_ref[...])
-        rows = rows.astype(BF16)
-        for zz in range(Z):
-            feats[zz] = rows[:, zz * fw:(zz + 1) * fw].reshape(T, M * share, fw)
+        for k in range(1, S):
+            where = lax.rem(s + S - k, S)
+            there = sall.at[pl.ds(1, Z - 1), :, :, :, scols(where)]
+            remote(there, there, fp_s.at[k - 1], fp_r.at[k - 1], (where, c, z)).wait_recv()
+        load_head.wait()
+
+        def one(k, carry):
+            rows = layer_norm(sall[k].astype(F32).reshape(T * M * share, sw), sgain_ref[...])
+            rows = rows.astype(BF16)
+            for zz in range(Z):
+                def own(zz=zz):
+                    fown[k] = rows[:, zz * fw:(zz + 1) * fw].reshape(T, M * share, fw)
+                pl.when(z == zz)(own)
+            pred[k] = jnp.dot(rows, whead[...], preferred_element_type=F32).reshape(
+                T, M, share, block
+            )
+            return carry
+
+        lax.fori_loop(0, Z, one, 0)
+
+    def spread(t):
+        def take():
+            there = tbuf.at[t, c, 0]
+            remote(there, there, tg_s.at[t, 0], tg_r.at[t], (root, c, z)).wait_recv()
+        pl.when(s != root)(take)
         for k in range(1, Z):
             def build(k=k):
-                to = zmod(z + k)
-                return remote(feats.at[to], ffull.at[z], fe_s.at[k - 1], fe_r.at[k - 1], (s, c, to))
+                return remote(tbuf.at[t, c, 0], tbuf.at[t, c, k], er_s.at[t, k - 1],
+                              er_r.at[t, k - 1], (s, c, zmod(z + k)))
             post(True, build)
-        ffull[z] = feats[z]
-        load_head.wait()
-        pred[...] = jnp.dot(rows, whead[...], preferred_element_type=F32).reshape(
-            T, M, share, block
-        )
-
-    def errors(t):
-        for cs in range(M):
-            def take(cs=cs):
-                there = tbuf.at[t, cs]
-                remote(there, there, tg_s.at[t, 0], tg_r.at[t, cs], (root, cs, z)).wait_recv()
-            pl.when(jnp.logical_or(s != root, c != cs))(take)
-        err = (pred[t] - tbuf[t].astype(F32)) * (2.0 / tokens)
-        errfull[t, z] = err.reshape(M * share, block).astype(BF16)
-        for k in range(1, Z):
-            def build(k=k):
-                own = errfull.at[t, z]
-                return remote(own, own, er_s.at[t, k - 1], er_r.at[t, k - 1],
-                              (s, c, zmod(z + k)))
-            post(True, build)
+
+    def relay(t):
+        for k in range(Z):
+            there = tbuf.at[t, c, k]
+            if k:
+                remote(there, there, er_s.at[t, k - 1], er_r.at[t, k - 1],
+                       (s, c, zmod(z - k))).wait_recv()
+            for dm in range(1, M):
+                def build(k=k, dm=dm):
+                    there = tbuf.at[t, c, k]
+                    return remote(there, there, ml_s.at[t, dm - 1, k], ml_r.at[t, dm - 1, k],
+                                  (s, lax.rem(c + dm, M), z))
+                post(True, build)
 
     def gradient(t):
-        for k in range(1, Z):
-            there = errfull.at[t, zmod(z - k)]
-            remote(there, there, er_s.at[t, k - 1], er_r.at[t, k - 1],
-                   (s, c, zmod(z - k))).wait_recv()
+        for dm in range(1, M):
+            for k in range(Z):
+                who = lax.rem(c + M - dm, M)
+                there = tbuf.at[t, who, k]
+                remote(there, there, ml_s.at[t, dm - 1, k], ml_r.at[t, dm - 1, k],
+                       (s, who, z)).wait_recv()
+
+        def one(k, carry):
+            err = (pred[k, t] - tbuf[t, :, k].astype(F32)) * (2.0 / tokens)
+            errs[k] = err.reshape(M * share, block).astype(BF16)
+            return carry
+
+        lax.fori_loop(0, Z, one, 0)
         term = lax.dot_general(
-            ffull[:, t].reshape(Z * M * share, fw), errfull[t].reshape(Z * M * share, block),
+            fown[:, t].reshape(Z * M * share, fw), errs[...].reshape(Z * M * share, block),
             (((0,), (0,)), ((), ())), preferred_element_type=F32,
         )
         if t == 0:
             grad_ref[...] = term
         else:
             grad_ref[...] += term
-
-    def take_feats():
-        for k in range(1, Z):
-            there = ffull.at[zmod(z - k)]
-            remote(there, there, fe_s.at[k - 1], fe_r.at[k - 1], (s, c, zmod(z - k))).wait_recv()
 
     def gather_state(t, active):
         def piece(r, origin):
@@ -249,7 +291,7 @@
             load_qkv.wait()
         rows = normed[...]
         query, keys, values = [
-            jnp.dot(rows, wqkv[:, j * wid:(j + 1) * wid], preferred_element_type=F32).astype(BF16)
+            jnp.dot(rows, wqkv[j], preferred_element_type=F32).astype(BF16)
             for j in range(3)
         ]
         crops = jnp.broadcast_to(seg_ref[s - t].astype(F32), (tokens, tokens))
@@ -309,21 +351,14 @@
                 remote(there, there, ro_s.at[t, k - 1], ro_r.at[t, k - 1],
                        (s, c, zmod(z - k))).wait_recv()
             tg[t] = layer_norm(fin[t], fgain_ref[...]).astype(BF16)
-            tbuf[t, c] = tg[t, :, root * block:(root + 1) * block]
+            tbuf[t, c, 0] = tg[t, :, root * block:(root + 1) * block]
 
         pl.when(s == root)(rows)
-        for to in range(S):
-            for dm in range(M):
-                if to == root and dm == 0:
-                    continue
-
-                def build(to=to, dm=dm):
-                    return remote(
-                        tg.at[t, :, to * block:(to + 1) * block], tbuf.at[t, c],
-                        tg_s.at[t, to * M + dm], tg_r.at[t, c],
-                        (jnp.int32(to), lax.rem(c + dm, M), z),
-                    )
-                post(s == root, build)
+        for to in range(root):
+            def build(to=to):
+                return remote(tg.at[t, :, to * block:(to + 1) * block], tbuf.at[t, c, 0],
+                              tg_s.at[t, to], tg_r.at[t], (jnp.int32(to), c, z))
+            post(s == root, build)
 
     for t in range(T):
         active = True if t == 0 else s >= t
@@ -331,22 +366,32 @@
             mixing(0)
         else:
             gather_state(t, active)
+            if t == 1:
+                pass_rows()
+            else:
+                relay(t - 2)
+                spread(t - 1)
             pl.when(active)(functools.partial(mixing, t))
         send_mixed(t, active)
         if t == 0:
-            student()
+            spread_rows()
             gather_wo()
             project(0)
         else:
-            errors(t - 1)
+            if t == 1:
+                spread(0)
+            if t == T - 1:
+                relay(t - 1)
+                student()
             pl.when(active)(functools.partial(project, t))
         send_state(t, active)
+        if t == T - 1:
+            for before in range(t):
+                gradient(before)
         finish(t)
 
-    take_feats()
-    for t in range(T - 1):
-        gradient(t)
-    errors(T - 1)
+    spread(T - 1)
+    relay(T - 1)
     gradient(T - 1)
 
     def arrived():
@@ -392,7 +437,7 @@
             in_specs=[vmem, vmem, vmem, hbm, hbm, vmem, vmem, vmem, hbm],
             out_specs=(vmem, vmem),
             scratch_shapes=[
-                pltpu.VMEM((model, 3 * wid), BF16),
+                pltpu.VMEM((3, model, wid), BF16),
                 pltpu.VMEM((Z * wid, cw), BF16),
                 pltpu.VMEM((sw, block), BF16),
                 pltpu.VMEM((tokens, model), BF16),
@@ -402,12 +447,12 @@
                 pltpu.VMEM((T, Z, share, cw), BF16),
                 pltpu.VMEM((T, share, model), BF16),
                 pltpu.VMEM((T, share, model), BF16),
-                pltpu.VMEM((T, M, share, block), BF16),
+                pltpu.VMEM((T, M, Z, share, block), BF16),
                 pltpu.VMEM((share, model), BF16),
+                pltpu.VMEM((Z, T, M, share, sw), BF16),
+                pltpu.VMEM((Z, T, M, share, block), F32),
                 pltpu.VMEM((Z, T, M * share, fw), BF16),
-                pltpu.VMEM((T, M, share, block), F32),
-                pltpu.VMEM((Z, T, M * share, fw), BF16),
-                pltpu.VMEM((T, Z, M * share, block), BF16),
+                pltpu.VMEM((Z, M * share, block), BF16),
                 dma((3,)),
                 dma((K,)), dma((K,)), dma((K,)), dma((K,)),
                 dma((T, K)), dma((T, K)),
@@ -416,15 +461,16 @@
                 dma((T - 1, K, R)), dma((T - 1, K, R)),
                 dma((T, K)), dma((T, K)),
                 dma((Z,)), dma((Z,)),
-                dma((T, S * M)), dma((T, M)),
-                dma((K,)), dma((K,)),
+                dma((T, S)), dma((T,)),
+                dma((K,)), dma((K,)), dma((S,)), dma((S,)),
                 dma((T, K)), dma((T, K)),
+                dma((T, M, Z)), dma((T, M, Z)),
             ],
             compiler_params=pltpu.CompilerParams(
                 collective_id=0, has_side_effects=True, vmem_limit_bytes=58 << 20
             ),
         )(
-            in_flight[0, 0], segments, norm_gain, w_qkv[0].reshape(model, -1), w_out[0],
+            in_flight[0, 0], segments, norm_gain, jnp.transpose(w_qkv[0], (1, 0, 2)), w_out[0],
             final_gain[None], student_rows[0], student_gain, w_head[0],
         )
         return adv[None, None], grad[None]

time: 172 us -> 140 us (0.81); the launches traced: 170 us -> 140 us
  local copies, waits for them, and re-layouts: 21.4 us -> 3.98 us
  Pallas kernels: 148 us -> 136 us
    pallas_call x1, Pallas kernels: 148 us -> 136 us  [on_device(): pl.pallas_call(functools.partial(window_kernel, S, M, Z, T, R), out_shape...]
    unnamed x3 -> x2, local copies, waits for them, and re-layouts: 12.7 us -> 3.98 us
    another operation x1 -> x0, local copies, waits for them, and re-layouts: 8.67 us -> none  [on_device(): w_qkv[0].reshape(model, -1)]
where the time goes in v2:
time: 140 us
  Pallas kernels  136 us (97%)
  local copies, waits for them, and re-layouts  3.98 us (3%)
    pallas_call x1, Pallas kernels, on_device(): pl.pallas_call(functools.partial(window_kernel, S, M, Z, T, R), out_shape...  136 us
    unnamed x2, local copies, waits for them, and re-layouts  3.98 us

profile of v2, /device:TPU:1, one launch (start us, length us, event | category | flops | bytes accessed | tf_op | source)
XLA Modules:
  0.0 140.1 jit_solution(12333558695064206357)
XLA Ops:
  0.6 135.5 %shard_map.104 = (bf16[32,4096]{1,0:T(8,128)(2,1)}, f32[256,1024]{1,0:T(8,128)}) custom-call(bf16[128,4096]{1,0:T(8,128)(2,1)} %bitcast.13, s32[4,1,128]{2,1,0:T(1,128)} %seg_ref.1, f32[1,4096]{1,0:T(1,128)} %gain_ref.1, bf16[3,4096,256]{2,1,0:T(8,128)(2,1)} %bitcast.10, bf16[256,4096]{1,0:T(8,128)(2,1)} %bitcast.11, f32[1,4096]{1,0:T(1,128)} %bitcast.17, ...), custom_call_target="tpu_custom_call" | custom-call | tf_op jit(solution)/shard_map/pallas_call | solution.py:431
  136.2 1.7 %copy.13 = bf16[1,1,32,4096]{3,2,1,0:T(8,128)(2,1)} copy(bf16[1,1,32,4096]{3,2,1,0:T(8,128)(2,1)} %bitcast.16) | data formatting | bytes 524288
  137.8 2.3 %copy.14 = f32[1,256,1024]{2,1,0:T(8,128)} copy(f32[1,256,1024]{2,1,0:T(8,128)} %bitcast.14) | data formatting | bytes 2097152

commit v3 on v2

--- a/solution.py
+++ b/solution.py
@@ -166,13 +166,14 @@
                               (lax.rem(s + k, S), c, z))
             post(True, build)
 
-    def student():
+    def take_rows():
         for k in range(1, S):
             where = lax.rem(s + S - k, S)
             there = sall.at[pl.ds(1, Z - 1), :, :, :, scols(where)]
             remote(there, there, fp_s.at[k - 1], fp_r.at[k - 1], (where, c, z)).wait_recv()
         load_head.wait()
 
+    def student(low, high):
         def one(k, carry):
             rows = layer_norm(sall[k].astype(F32).reshape(T * M * share, sw), sgain_ref[...])
             rows = rows.astype(BF16)
@@ -185,7 +186,7 @@
             )
             return carry
 
-        lax.fori_loop(0, Z, one, 0)
+        lax.fori_loop(low, high, one, 0)
 
     def spread(t):
         def take():
@@ -234,7 +235,7 @@
         else:
             grad_ref[...] += term
 
-    def gather_state(t, active):
+    def gather_state(t, active, between):
         def piece(r, origin):
             return xfull.at[t - 1, pl.ds(r * step_rows, step_rows), cols(origin)]
 
@@ -264,6 +265,7 @@
             pl.when(active)(first)
             post(jnp.logical_and(active, z < Z - 1), functools.partial(to_right, r, 0))
             post(jnp.logical_and(active, z > 0), functools.partial(to_left, r, 0))
+        between()
         for k in range(1, Z):
             for r in range(R):
                 pl.when(jnp.logical_and(active, z >= k))(functools.partial(right_from, r, k))
@@ -365,10 +367,13 @@
         if t == 0:
             mixing(0)
         else:
-            gather_state(t, active)
-            if t == 1:
-                pass_rows()
-            else:
+            def between(t=t):
+                finish(t - 1)
+                if t == 1:
+                    pass_rows()
+
+            gather_state(t, active, between)
+            if t > 1:
                 relay(t - 2)
                 spread(t - 1)
             pl.when(active)(functools.partial(mixing, t))
@@ -380,16 +385,18 @@
         else:
             if t == 1:
                 spread(0)
+                take_rows()
+                student(0, Z // 2)
             if t == T - 1:
                 relay(t - 1)
-                student()
+                student(Z // 2, Z)
             pl.when(active)(functools.partial(project, t))
         send_state(t, active)
         if t == T - 1:
             for before in range(t):
                 gradient(before)
-        finish(t)
-
+
+    finish(T - 1)
     spread(T - 1)
     relay(T - 1)
     gradient(T - 1)

time: 140 us -> 142 us (1.014)
    pallas_call x1, Pallas kernels: 136 us -> 137 us  [on_device(): pl.pallas_call(functools.partial(window_kernel, S, M, Z, T, R), out_shape...]
where the time goes in v3:
time: 142 us
  Pallas kernels  137 us (96%)
  local copies, waits for them, and re-layouts  3.98 us (3%)
    pallas_call x1, Pallas kernels, on_device(): pl.pallas_call(functools.partial(window_kernel, S, M, Z, T, R), out_shape...  137 us
    unnamed x2, local copies, waits for them, and re-layouts  3.98 us

profile of v3, /device:TPU:1, one launch (start us, length us, event | category | flops | bytes accessed | tf_op | source)
XLA Modules:
  0.0 142.0 jit_solution(12939798007890198975)
XLA Ops:
  0.6 137.4 %shard_map.104 = (bf16[32,4096]{1,0:T(8,128)(2,1)}, f32[256,1024]{1,0:T(8,128)}) custom-call(bf16[128,4096]{1,0:T(8,128)(2,1)} %bitcast.13, s32[4,1,128]{2,1,0:T(1,128)} %seg_ref.1, f32[1,4096]{1,0:T(1,128)} %gain_ref.1, bf16[3,4096,256]{2,1,0:T(8,128)(2,1)} %bitcast.10, bf16[256,4096]{1,0:T(8,128)(2,1)} %bitcast.11, f32[1,4096]{1,0:T(1,128)} %bitcast.17, ...), custom_call_target="tpu_custom_call" | custom-call | tf_op jit(solution)/shard_map/pallas_call | solution.py:438
  138.0 1.7 %copy.13 = bf16[1,1,32,4096]{3,2,1,0:T(8,128)(2,1)} copy(bf16[1,1,32,4096]{3,2,1,0:T(8,128)(2,1)} %bitcast.16) | data formatting | bytes 524288
  139.7 2.3 %copy.14 = f32[1,256,1024]{2,1,0:T(8,128)} copy(f32[1,256,1024]{2,1,0:T(8,128)} %bitcast.14) | data formatting | bytes 2097152

commit v4 on v3

--- a/solution.py
+++ b/solution.py
@@ -367,13 +367,10 @@
         if t == 0:
             mixing(0)
         else:
-            def between(t=t):
-                finish(t - 1)
-                if t == 1:
-                    pass_rows()
-
-            gather_state(t, active, between)
-            if t > 1:
+            gather_state(t, active, functools.partial(finish, t - 1))
+            if t == 1:
+                pass_rows()
+            else:
                 relay(t - 2)
                 spread(t - 1)
             pl.when(active)(functools.partial(mixing, t))
@@ -385,11 +382,10 @@
         else:
             if t == 1:
                 spread(0)
-                take_rows()
-                student(0, Z // 2)
             if t == T - 1:
                 relay(t - 1)
-                student(Z // 2, Z)
+                take_rows()
+                student(0, Z)
             pl.when(active)(functools.partial(project, t))
         send_state(t, active)
         if t == T - 1:

time: 142 us -> 141 us (level)
    pallas_call x1, Pallas kernels: 137 us -> 136 us  [on_device(): pl.pallas_call(functools.partial(window_kernel, S, M, Z, T, R), out_shape...]
where the time goes in v4:
time: 141 us; the launch traced here: 140 us
  Pallas kernels  136 us (96%)
  local copies, waits for them, and re-layouts  3.98 us (3%)
    pallas_call x1, Pallas kernels, on_device(): pl.pallas_call(functools.partial(window_kernel, S, M, Z, T, R), out_shape...  136 us
    unnamed x2, local copies, waits for them, and re-layouts  3.98 us

profile of v4, /device:TPU:1, one launch (start us, length us, event | category | flops | bytes accessed | tf_op | source)
XLA Modules:
  0.0 140.3 jit_solution(10479540669957019539)
XLA Ops:
  0.6 135.7 %shard_map.104 = (bf16[32,4096]{1,0:T(8,128)(2,1)}, f32[256,1024]{1,0:T(8,128)}) custom-call(bf16[128,4096]{1,0:T(8,128)(2,1)} %bitcast.13, s32[4,1,128]{2,1,0:T(1,128)} %seg_ref.1, f32[1,4096]{1,0:T(1,128)} %gain_ref.1, bf16[3,4096,256]{2,1,0:T(8,128)(2,1)} %bitcast.10, bf16[256,4096]{1,0:T(8,128)(2,1)} %bitcast.11, f32[1,4096]{1,0:T(1,128)} %bitcast.17, ...), custom_call_target="tpu_custom_call" | custom-call | tf_op jit(solution)/shard_map/pallas_call | solution.py:434
  136.4 1.7 %copy.13 = bf16[1,1,32,4096]{3,2,1,0:T(8,128)(2,1)} copy(bf16[1,1,32,4096]{3,2,1,0:T(8,128)(2,1)} %bitcast.16) | data formatting | bytes 524288
  138.0 2.3 %copy.14 = f32[1,256,1024]{2,1,0:T(8,128)} copy(f32[1,256,1024]{2,1,0:T(8,128)} %bitcast.14) | data formatting | bytes 2097152
